TPU v7x, 32 devices: a whole 2x2x4 slice. The times are simulated.
32 devices in a mesh: grp: 2 (over x), ctx: 16 (over z, y, core).
Axes of the slice: x: 2, y: 2, z: 4, core: 2. Of those that a mesh axis runs over, the one named last changes fastest.
Arguments:
- queries: bfloat16 [2, 24, 64, 576], P('grp', None, 'ctx'), parts along dimension 0, may hold values from -40 to 40
- cache: bfloat16 [2, 8192, 576], P('grp', 'ctx'), parts along dimension 0, may hold values from -6 to 6
- draft_latent: bfloat16 [2, 24, 576], P('grp'), parts along dimension 0, may hold values from -9 to 9
- lengths: int32 [2], P('grp'), parts along dimension 0, may hold values from 4096 to 8192
- parents: int32 [2, 24], P('grp'), parts along dimension 0, may hold values from -1 to 22, as said below
- value_up: bfloat16 [64, 512, 128], P('ctx'), may hold values from -0.25 to 0.25
- out_proj: bfloat16 [8192, 7168], P('ctx'), may hold values from -0.09375 to 0.09375
Outputs:
- attended: bfloat16 [48, 7168], P('grp', 'ctx'), parts along dimension 0
There are 2 independent parts, one for each index of `grp`. A program takes and returns all parts, laid end to end along the dimension named above; an argument that names none is the same for every part. Nothing has to cross between parts.
Inputs may be any that keep to these rules, and one draw needn't show every extreme that they name: parents[r, 0] = -1 and 0 <= parents[r, i] < i for i >= 1.
All inputs are finite; a program needn't handle non-finite values.
Results may differ from a plain program's by a relative error of at most 0.007.
Values may be sent and summed in bfloat16 or wider, within the bound.
A program may use at most 64 MiB of HBM per device.

v0:
```python
import math
import jax
import jax.numpy as jnp
from jax import lax
from jax.sharding import PartitionSpec as P

yarn_factor = 1.0 + 0.1 * math.log(32.0)
score_scale = yarn_factor * yarn_factor / math.sqrt(192.0)
neg_fill = -1e30


def tree_reach(parents):
    drafts = parents.shape[1]
    order = jnp.arange(drafts, dtype=jnp.int32)
    adjacent = (parents[:, :, None] == order[None, None, :]).astype(jnp.float32)
    ident = jnp.broadcast_to(jnp.eye(drafts, dtype=jnp.float32), adjacent.shape)

    def extend(step, reach):
        grown = ident + jnp.einsum("rij,rjk->rik", adjacent, reach, precision=lax.Precision.HIGHEST)
        return jnp.minimum(grown, 1.0)

    return lax.fori_loop(0, drafts, extend, ident) > 0.5


def block_state(rows, keys, valid, latent_width):
    scores = (
        lax.dot_general(
            rows, keys, (((2,), (2,)), ((0,), (0,))), preferred_element_type=jnp.float32
        )
        * score_scale
    )
    masked = jnp.where(valid, scores, neg_fill)
    top = jnp.max(masked, axis=2)
    weights = jnp.where(valid, jnp.exp(masked - top[:, :, None]), 0.0).astype(jnp.bfloat16)
    numer = lax.dot_general(
        weights, keys, (((2,), (1,)), ((0,), (0,))), preferred_element_type=jnp.float32
    )
    total = jnp.sum(weights.astype(jnp.float32), axis=2)
    return (numer[:, :, :latent_width], top, total)


def join(first, second):
    best = jnp.maximum(first[1], second[1])
    factor_a = jnp.exp(first[1] - best)
    factor_b = jnp.exp(second[1] - best)
    return (
        first[0] * factor_a[..., None] + second[0] * factor_b[..., None],
        best,
        first[2] * factor_a + second[2] * factor_b,
    )


def on_device(queries, cache, draft_latent, lengths, parents, value_up, out_proj):
    requests, drafts, heads_here, width = queries.shape
    block_len = cache.shape[1]
    latent_width = value_up.shape[1]
    myself = lax.axis_index("ctx")
    positions = myself * block_len + jnp.arange(block_len, dtype=jnp.int32)
    live = (positions[None, :] < lengths[:, None])[:, None, :]
    own_rows = queries.reshape(requests, drafts * heads_here, width)
    every = lax.all_gather(queries, "ctx", axis=2, tiled=True)
    heads = every.shape[2]
    rows = every.reshape(requests, drafts * heads, width)
    numer, top, total = block_state(rows, cache, live, latent_width)
    numer = numer.reshape(1, requests, drafts, heads, latent_width)
    top = top.reshape(1, requests, drafts, heads)
    total = total.reshape(1, requests, drafts, heads)
    numers, tops, totals = (
        lax.all_to_all(numer, "ctx", split_axis=3, concat_axis=0, tiled=True),
        lax.all_to_all(top, "ctx", split_axis=3, concat_axis=0, tiled=True),
        lax.all_to_all(total, "ctx", split_axis=3, concat_axis=0, tiled=True),
    )
    best = jnp.max(tops, axis=0)
    factor = jnp.exp(tops - best[None])
    context = (
        jnp.sum(numers * factor[..., None], axis=0).reshape(
            requests, drafts * heads_here, latent_width
        ),
        best.reshape(requests, drafts * heads_here),
        jnp.sum(totals * factor, axis=0).reshape(requests, drafts * heads_here),
    )
    reach = tree_reach(parents)
    tree = jnp.repeat(reach, heads_here, axis=1)
    whole = join(context, block_state(own_rows, draft_latent, tree, latent_width))
    latent_out = (whole[0] / whole[2][..., None]).astype(jnp.bfloat16)
    latent_out = latent_out.reshape(requests, drafts, heads_here, latent_width)
    values = jnp.einsum(
        "rdhl,hlv->rdhv", latent_out, value_up, preferred_element_type=jnp.float32
    ).astype(jnp.bfloat16)
    flat = values.reshape(requests * drafts, heads_here * value_up.shape[2])
    partial_value = jnp.dot(flat, out_proj, preferred_element_type=jnp.float32)
    return lax.psum_scatter(partial_value, "ctx", scatter_dimension=1, tiled=True).astype(
        jnp.bfloat16
    )


def solution(mesh):
    in_specs = (
        P("grp", None, "ctx", None),
        P("grp", "ctx", None),
        P("grp", None, None),
        P("grp"),
        P("grp", None),
        P("ctx", None, None),
        P("ctx", None),
    )
    out_specs = P("grp", "ctx")
    return jax.shard_map(
        on_device, mesh=mesh, in_specs=in_specs, out_specs=out_specs, check_vma=False
    )
```

profile of v0, /device:TPU:0, one launch (start us, length us, event | category | flops | bytes accessed | tf_op | source)
XLA Modules:
  0.0 251.4 jit_solution(7607140488094526132)
XLA Ops:
  6.5 1.6 copy.40
  8.9 44.5 %all-gather.2.cloned.1.call-done = bf16[1,24,64,576]{3,1,0,2:T(8,128)(2,1)} async-done(((bf16[1,24,4,576]{3,1,0,2:T(8,128)(2,1)}), bf16[1,24,64,576]{3,1,0,2:T(8,128)(2,1)}) %all-gather.2.cloned.1.call-update) | async-done | bytes 1769488 | tf_op jit(solution)/shard_map/all_gather | solution.py:61
  53.4 1.9 copy.41
  55.3 1.5 fusion.29
  56.8 1.7 copy-done.1
  58.5 0.6 convert_reduce_fusion
  59.1 0.7 copy.49
  59.8 3.5 %all-to-all-start.2 = ((f32[1,1,24,64]{2,1,0,3:T(1,128)}), f32[1,1,24,64]{2,1,0,3:T(1,128)S(1)}, u32[]{:S(2)}, u32[]{:S(2)}) async-start(f32[1,1,24,64]{2,1,0,3:T(1,128)} %copy.49), calls=%async_computation.2 | async-start | bytes 65536 | tf_op jit(solution)/shard_map/all_to_all | solution.py:71
  63.4 0.7 copy.44
  64.1 5.9 %all-to-all-done.2 = f32[1,1,24,64]{2,1,0,3:T(1,128)S(1)} async-done(((f32[1,1,24,64]{2,1,0,3:T(1,128)}), f32[1,1,24,64]{2,1,0,3:T(1,128)S(1)}, u32[]{:S(2)}, u32[]{:S(2)}) %all-to-all-start.2) | async-done | bytes 6176 | tf_op jit(solution)/shard_map/all_to_all | solution.py:71
  69.9 3.5 %all-to-all-start.1 = ((f32[1,1,24,64]{2,1,0,3:T(1,128)}), f32[1,1,24,64]{2,1,0,3:T(1,128)S(1)}, u32[]{:S(2)}, u32[]{:S(2)}) async-start(f32[1,1,24,64]{2,1,0,3:T(1,128)} %copy.44), calls=%async_computation.1 | async-start | bytes 65536 | tf_op jit(solution)/shard_map/all_to_all | solution.py:70
  73.4 3.1 %convolution_bitcast_fusion.1 = f32[1,1536,576]{1,2,0:T(8,128)S(1)} fusion(bf16[1,512,576]{1,2,0:T(8,128)(2,1)S(1)} %copy-done, f32[1536,512]{0,1:T(8,128)} %copy-done.1, f32[1536]{0:T(1024)S(1)} %get-tuple-element.49, pred[512]{0:T(512)(128)(4,1)S(1)} %add_compare_fusion), kind=kOutput, calls=%fused_computation.12 | convolution fusion | flops 908328960 | bytes 7281152 | tf_op jit(solution)/shard_map/dot_general | solution.py:35
  76.5 1.9 slice.8
  78.4 3.6 %copy.42 = f32[1,1536,512]{2,1,0:T(8,128)} copy(f32[1,1536,512]{1,2,0:T(8,128)} %slice.8) | data formatting | bytes 6291456 | tf_op jit(solution)/shard_map/slice | solution.py:39
  82.0 5.4 %copy.43 = f32[1,1,24,64,512]{4,2,1,0,3:T(8,128)} copy(f32[1,1,24,64,512]{4,3,2,1,0:T(8,128)} %bitcast.82) | data formatting | bytes 6291456 | tf_op jit(solution)/shard_map/reshape | solution.py:65
  87.4 6.2 %all-to-all-start = ((f32[1,1,24,64,512]{4,2,1,0,3:T(8,128)}), f32[1,1,24,64,512]{4,2,1,0,3:T(8,128)}, u32[]{:S(2)}, u32[]{:S(2)}) async-start(f32[1,1,24,64,512]{4,2,1,0,3:T(8,128)} %copy.43), calls=%async_computation | async-start | bytes 6291456 | tf_op jit(solution)/shard_map/all_to_all | solution.py:69
  93.7 5.8 %while.11 = (s32[]{:T(128)}, f32[1,24,24]{2,1,0:T(8,128)S(1)}, s32[24]{0:T(128)S(1)}, s32[]{:T(128)}) while((s32[]{:T(128)}, f32[1,24,24]{2,1,0:T(8,128)S(1)}, s32[24]{0:T(128)S(1)}, s32[]{:T(128)}) %tuple.32), condition=%wide.region_4.5_spmd.clone, body=%wide.region_3.4_spmd.clone.sunk | while | flops 169346 | bytes 9365 | solution.py:22
  93.7 0.2 fusion.39
  94.0 0.2 fusion.39
  94.2 0.2 fusion.39
  94.4 0.2 fusion.39
  94.7 0.2 fusion.39
  94.9 0.2 fusion.39
  95.7 0.2 fusion.39
  96.6 0.2 fusion.39
  97.6 0.2 fusion.39
  99.9 0.2 convolution_bitcast_fusion.2
  100.6 52.2 %all-to-all-done = f32[1,1,24,64,512]{4,2,1,0,3:T(8,128)} async-done(((f32[1,1,24,64,512]{4,2,1,0,3:T(8,128)}), f32[1,1,24,64,512]{4,2,1,0,3:T(8,128)}, u32[]{:S(2)}, u32[]{:S(2)}) %all-to-all-start) | async-done | bytes 3145760 | tf_op jit(solution)/shard_map/all_to_all | solution.py:69
  152.8 2.2 multiply_reduce_fusion
  155.6 7.8 %convolution_bitcast_fusion = f32[7168,24]{1,0:T(8,128)} fusion(bf16[512,7168]{1,0:T(8,128)(2,1)} %param.15, bf16[3,8,4,128]{3,2,1,0:T(4,128)(2,1)S(1)} %bitcast.90), kind=kOutput, calls=%fused_computation.11 | convolution fusion | flops 176160768 | bytes 8052736
  163.5 79.5 %reduce-scatter.4.cloned.1.call-done = f32[448,24]{1,0:T(8,128)} async-done(((f32[7168,24]{1,0:T(8,128)}), f32[448,24]{1,0:T(8,128)}) %reduce-scatter.4.cloned.1.call-update) | async-done | bytes 43024
  243.0 1.6 copy.54
  (80 shorter events, 4.8 us)
Async XLA Ops:
  6.5 48.7 %copy-start = (bf16[1,512,576]{1,2,0:T(8,128)(2,1)S(1)}, bf16[1,512,576]{1,2,0:T(8,128)(2,1)}, u32[]{:S(2)}) copy-start(bf16[1,512,576]{1,2,0:T(8,128)(2,1)} %param.10) | copy-start | bytes 1769476
  6.5 46.9 %all-gather.2.cloned.1.call-start = ((), (), s32[]{:S(2)}) async-start(), calls=%async_computation.4 | async-start | bytes 2088960 | tf_op jit(solution)/shard_map/all_gather | solution.py:61
  56.8 1.7 copy-start.1
  59.8 10.1 %all-to-all-start.2 = ((f32[1,1,24,64]{2,1,0,3:T(1,128)}), f32[1,1,24,64]{2,1,0,3:T(1,128)S(1)}, u32[]{:S(2)}, u32[]{:S(2)}) async-start(f32[1,1,24,64]{2,1,0,3:T(1,128)} %copy.49), calls=%async_computation.2 | async-start | bytes 65536 | tf_op jit(solution)/shard_map/all_to_all | solution.py:71
  69.9 17.4 %all-to-all-start.1 = ((f32[1,1,24,64]{2,1,0,3:T(1,128)}), f32[1,1,24,64]{2,1,0,3:T(1,128)S(1)}, u32[]{:S(2)}, u32[]{:S(2)}) async-start(f32[1,1,24,64]{2,1,0,3:T(1,128)} %copy.44), calls=%async_computation.1 | async-start | bytes 65536 | tf_op jit(solution)/shard_map/all_to_all | solution.py:70
  87.3 6.2 %copy-start.3 = (bf16[1,24,4,576]{3,2,1,0:T(4,128)(2,1)S(1)}, bf16[1,24,4,576]{3,2,1,0:T(4,128)(2,1)}, u32[]{:S(2)}) copy-start(bf16[1,24,4,576]{3,2,1,0:T(4,128)(2,1)} %param.9) | copy-start | bytes 331780
  87.4 6.3 %copy-start.5 = (s32[1,24]{1,0:T(1,128)S(1)}, s32[1,24]{1,0:T(1,128)}, u32[]{:S(2)}) copy-start(s32[1,24]{1,0:T(1,128)} %param.13) | copy-start | bytes 292
  87.4 12.3 %copy-start.4 = (bf16[1,24,576]{2,1,0:T(8,128)(2,1)S(1)}, bf16[1,24,576]{2,1,0:T(8,128)(2,1)}, u32[]{:S(2)}) copy-start(bf16[1,24,576]{2,1,0:T(8,128)(2,1)} %param.11) | copy-start | bytes 82948
  87.4 65.5 %all-to-all-start = ((f32[1,1,24,64,512]{4,2,1,0,3:T(8,128)}), f32[1,1,24,64,512]{4,2,1,0,3:T(8,128)}, u32[]{:S(2)}, u32[]{:S(2)}) async-start(f32[1,1,24,64,512]{4,2,1,0,3:T(8,128)} %copy.43), calls=%async_computation | async-start | bytes 6291456 | tf_op jit(solution)/shard_map/all_to_all | solution.py:69
  93.5 149.4 %reduce-scatter.4.cloned.1.call-start = ((), (), s32[]{:S(2)}) async-start(), calls=%async_computation.5 | async-start | bytes 3899392
  93.7 61.7 %copy-start.2 = (bf16[4,512,128]{2,1,0:T(8,128)(2,1)S(1)}, bf16[4,512,128]{2,1,0:T(8,128)(2,1)}, u32[]{:S(2)}) copy-start(bf16[4,512,128]{2,1,0:T(8,128)(2,1)} %param.14) | copy-start | bytes 1572868
Sparse Core Ops, SparseCore 0:
  9.6 43.7 all-gather.1
  163.6 79.3 reduce-scatter.3
where the time goes:
time: 252 us; the launch traced here: 251 us
  waiting for transfers between devices  182 us (72%)
  local copies, waits for them, and re-layouts  20 us (8%)
  matrix products  18 us (7%)
  between operations  14.3 us (6%)
  starting transfers between devices  13.2 us (5%)
  other arithmetic  2.99 us (1%)
    unnamed x3, waiting for transfers between devices  79.5 us
    all_to_all x1, waiting for transfers between devices, on_device(): lax.all_to_all(numer, 'ctx', split_axis=3, concat_axis=0, tiled=True)  52.2 us
    all_gather x1, waiting for transfers between devices, on_device(): every = lax.all_gather(queries, 'ctx', axis=2, tiled=True)  44.5 us
    unnamed x1, matrix products  7.84 us
    all_to_all x1, starting transfers between devices, on_device(): lax.all_to_all(numer, 'ctx', split_axis=3, concat_axis=0, tiled=True)  6.16 us
    all_to_all x1, waiting for transfers between devices, on_device(): lax.all_to_all(total, 'ctx', split_axis=3, concat_axis=0, tiled=True)  5.86 us
    slice x2, local copies, waits for them, and re-layouts, block_state(): return (numer[:, :, :latent_width], top, total)  5.45 us
    reshape x1, local copies, waits for them, and re-layouts, on_device(): numer = numer.reshape(1, requests, drafts, heads, latent_width)  5.38 us
  transfers between devices with their start and end apart: 5, of which 4 were waited for; matrix products, arithmetic and copies ran while one was open for 8% of the time, Pallas kernels for 0%

commit v1 on v0

--- a/solution.py
+++ b/solution.py
@@ -66,7 +66,10 @@
     top = top.reshape(1, requests, drafts, heads)
     total = total.reshape(1, requests, drafts, heads)
     numers, tops, totals = (
-        lax.all_to_all(numer, "ctx", split_axis=3, concat_axis=0, tiled=True),
+        jnp.concatenate(
+            lax.all_to_all(jnp.stack(jnp.split(numer, lax.axis_size("ctx"), axis=3)), "ctx", 0, 0),
+            axis=0,
+        ),
         lax.all_to_all(top, "ctx", split_axis=3, concat_axis=0, tiled=True),
         lax.all_to_all(total, "ctx", split_axis=3, concat_axis=0, tiled=True),
     )

time: 252 us -> 278 us (1.10)
  local copies, waits for them, and re-layouts: 20 us -> 42.4 us
    unnamed x15 -> x30, local copies, waits for them, and re-layouts: 4.94 us -> 29.1 us
    reshape x1 -> x0, local copies, waits for them, and re-layouts: 5.38 us -> none  [on_device(): numer = numer.reshape(1, requests, drafts, heads, latent_width)]
  transfers between devices with their start and end apart: 5 -> 5, of which waited for: 4 -> 4; matrix products, arithmetic and copies ran while one was open for 8% -> 15% of each run, Pallas kernels for 0% -> 0%
where the time goes in v1:
time: 278 us; the launch traced here: 277 us
  waiting for transfers between devices  181 us (65%)
  local copies, waits for them, and re-layouts  42.4 us (15%)
  matrix products  19.6 us (7%)
  between operations  14.3 us (5%)
  starting transfers between devices  14 us (5%)
  other arithmetic  5.16 us (2%)
    unnamed x3, waiting for transfers between devices  79.4 us
    all_to_all x1, waiting for transfers between devices, on_device(): lax.all_to_all(jnp.stack(jnp.split(numer, lax.axis_size('ctx'), axis=3)),...  52 us
    all_gather x1, waiting for transfers between devices, on_device(): every = lax.all_gather(queries, 'ctx', axis=2, tiled=True)  44.5 us
    unnamed x30, local copies, waits for them, and re-layouts  29.1 us
    unnamed x1, matrix products  7.84 us
    slice x2, local copies, waits for them, and re-layouts, block_state(): return (numer[:, :, :latent_width], top, total)  7.31 us
    all_to_all x1, starting transfers between devices, on_device(): lax.all_to_all(total, 'ctx', split_axis=3, concat_axis=0, tiled=True)  5.99 us
  transfers between devices with their start and end apart: 5, of which 4 were waited for; matrix products, arithmetic and copies ran while one was open for 15% of the time, Pallas kernels for 0%

profile of v1, /device:TPU:0, one launch (start us, length us, event | category | flops | bytes accessed | tf_op | source)
XLA Modules:
  0.0 277.1 jit_solution(878397136023374847)
XLA Ops:
  8.9 44.5 %all-gather.2.cloned.1.call-done = bf16[1,24,64,576]{3,1,0,2:T(8,128)(2,1)} async-done(((bf16[1,24,4,576]{3,1,0,2:T(8,128)(2,1)}), bf16[1,24,64,576]{3,1,0,2:T(8,128)(2,1)}) %all-gather.2.cloned.1.call-update) | async-done | bytes 1769488 | tf_op jit(solution)/shard_map/all_gather | solution.py:61
  53.4 1.9 copy.40
  55.3 3.2 %fusion.46 = (f32[1536]{0:T(1024)S(1)}, f32[1536,512]{0,1:T(8,128)}) fusion(bf16[1536,576]{1,0:T(8,128)(2,1)S(1)} %bitcast.161, bf16[1,512,576]{1,2,0:T(8,128)(2,1)S(1)} %copy-done, pred[512]{0:T(512)(128)(4,1)S(1)} %add_compare_fusion), kind=kOutput, calls=%fused_computation.81 | convolution fusion | flops 908327424 | bytes 5511680 | tf_op jit(solution)/shard_map/dot_general | solution.py:27
  58.5 2.6 convert_reduce_fusion
  61.4 3.0 %convolution_bitcast_fusion.1 = f32[1,1536,576]{1,2,0:T(8,128)} fusion(bf16[1,512,576]{1,2,0:T(8,128)(2,1)S(1)} %copy-done, f32[1536,512]{0,1:T(8,128)S(1)} %copy-done.1, f32[1536]{0:T(1024)S(1)} %get-tuple-element.49, pred[512]{0:T(512)(128)(4,1)S(1)} %add_compare_fusion), kind=kOutput, calls=%fused_computation.12 | convolution fusion | flops 908328960 | bytes 7281152 | tf_op jit(solution)/shard_map/dot_general | solution.py:35
  65.0 3.5 %all-to-all-start.1 = ((f32[1,1,24,64]{2,1,0,3:T(1,128)}), f32[1,1,24,64]{2,1,0,3:T(1,128)S(1)}, u32[]{:S(2)}, u32[]{:S(2)}) async-start(f32[1,1,24,64]{2,1,0,3:T(1,128)} %copy.42), calls=%async_computation.1 | async-start | bytes 65536 | tf_op jit(solution)/shard_map/all_to_all | solution.py:73
  68.5 3.8 %slice.8 = f32[1,1536,512]{1,2,0:T(8,128)} slice(f32[1,1536,576]{1,2,0:T(8,128)} %convolution_bitcast_fusion.1), slice={[0:1], [0:1536], [0:512]} | slice | bytes 6291456 | tf_op jit(solution)/shard_map/slice | solution.py:39
  72.3 3.5 %copy.41 = f32[1,1536,512]{2,1,0:T(8,128)} copy(f32[1,1536,512]{1,2,0:T(8,128)} %slice.8) | data formatting | bytes 6291456 | tf_op jit(solution)/shard_map/slice | solution.py:39
  75.9 1.7 fusion.33
  77.6 1.7 fusion.32
  79.3 1.7 fusion.31
  81.0 1.7 fusion.30
  82.7 1.7 fusion.29
  84.4 1.7 fusion.28
  86.1 1.7 fusion.27
  87.8 1.7 fusion.26
  89.5 1.7 fusion.25
  91.2 1.7 fusion.24
  92.9 1.7 fusion.23
  94.6 1.7 fusion.22
  96.3 1.7 fusion.21
  98.0 1.7 fusion.20
  99.7 1.7 fusion.19
  102.2 6.0 %all-to-all-start.2 = ((f32[1,1,24,64]{2,1,0,3:T(1,128)}), f32[1,1,24,64]{2,1,0,3:T(1,128)S(1)}, u32[]{:S(2)}, u32[]{:S(2)}) async-start(f32[1,1,24,64]{2,1,0,3:T(1,128)} %copy.47), calls=%async_computation.2 | async-start | bytes 65536 | tf_op jit(solution)/shard_map/all_to_all | solution.py:74
  108.2 1.7 fusion.18
  110.0 4.9 %all-to-all-done.2 = f32[1,1,24,64]{2,1,0,3:T(1,128)S(1)} async-done(((f32[1,1,24,64]{2,1,0,3:T(1,128)}), f32[1,1,24,64]{2,1,0,3:T(1,128)S(1)}, u32[]{:S(2)}, u32[]{:S(2)}) %all-to-all-start.2) | async-done | bytes 6176 | tf_op jit(solution)/shard_map/all_to_all | solution.py:74
  114.8 4.5 %all-to-all-start = ((f32[16,1,1,24,4,512]{5,4,3,2,1,0:T(4,128)}), f32[16,1,1,24,4,512]{5,4,3,2,1,0:T(4,128)}, u32[]{:S(2)}, u32[]{:S(2)}) async-start(f32[16,1,1,24,4,512]{5,4,3,2,1,0:T(4,128)} %fusion.18), calls=%async_computation | async-start | bytes 6291456 | tf_op jit(solution)/shard_map/all_to_all | solution.py:70
  119.5 5.8 %while.11 = (s32[]{:T(128)}, f32[1,24,24]{2,1,0:T(8,128)S(1)}, s32[24]{0:T(128)S(1)}, s32[]{:T(128)}) while((s32[]{:T(128)}, f32[1,24,24]{2,1,0:T(8,128)S(1)}, s32[24]{0:T(128)S(1)}, s32[]{:T(128)}) %tuple.32), condition=%wide.region_4.5_spmd.clone, body=%wide.region_3.4_spmd.clone.sunk | while | flops 169346 | bytes 9365 | solution.py:22
  126.6 52.0 %all-to-all-done = f32[16,1,1,24,4,512]{5,4,3,2,1,0:T(4,128)} async-done(((f32[16,1,1,24,4,512]{5,4,3,2,1,0:T(4,128)}), f32[16,1,1,24,4,512]{5,4,3,2,1,0:T(4,128)}, u32[]{:S(2)}, u32[]{:S(2)}) %all-to-all-start) | async-done | bytes 3145760 | tf_op jit(solution)/shard_map/all_to_all | solution.py:70
  178.6 2.3 fusion.11
  181.3 7.8 %convolution_bitcast_fusion = f32[7168,24]{1,0:T(8,128)} fusion(bf16[512,7168]{1,0:T(8,128)(2,1)} %param.15, bf16[3,8,4,128]{3,2,1,0:T(4,128)(2,1)S(1)} %bitcast.168), kind=kOutput, calls=%fused_computation.11 | convolution fusion | flops 176160768 | bytes 8052736
  189.2 79.4 %reduce-scatter.4.cloned.1.call-done = f32[448,24]{1,0:T(8,128)} async-done(((f32[7168,24]{1,0:T(8,128)}), f32[448,24]{1,0:T(8,128)}) %reduce-scatter.4.cloned.1.call-update) | async-done | bytes 43024
  (95 shorter events, 11.8 us)
Async XLA Ops:
  6.5 48.7 %copy-start = (bf16[1,512,576]{1,2,0:T(8,128)(2,1)S(1)}, bf16[1,512,576]{1,2,0:T(8,128)(2,1)}, u32[]{:S(2)}) copy-start(bf16[1,512,576]{1,2,0:T(8,128)(2,1)} %param.10) | copy-start | bytes 1769476
  6.5 46.9 %all-gather.2.cloned.1.call-start = ((), (), s32[]{:S(2)}) async-start(), calls=%async_computation.4 | async-start | bytes 2088960 | tf_op jit(solution)/shard_map/all_gather | solution.py:61
  58.5 2.8 %copy-start.1 = (f32[1536,512]{0,1:T(8,128)S(1)}, f32[1536,512]{0,1:T(8,128)}, u32[]{:S(2)}) copy-start(f32[1536,512]{0,1:T(8,128)} %get-tuple-element.50) | copy-start | bytes 9437188
  65.0 37.2 %all-to-all-start.1 = ((f32[1,1,24,64]{2,1,0,3:T(1,128)}), f32[1,1,24,64]{2,1,0,3:T(1,128)S(1)}, u32[]{:S(2)}, u32[]{:S(2)}) async-start(f32[1,1,24,64]{2,1,0,3:T(1,128)} %copy.42), calls=%async_computation.1 | async-start | bytes 65536 | tf_op jit(solution)/shard_map/all_to_all | solution.py:73
  102.2 12.6 %all-to-all-start.2 = ((f32[1,1,24,64]{2,1,0,3:T(1,128)}), f32[1,1,24,64]{2,1,0,3:T(1,128)S(1)}, u32[]{:S(2)}, u32[]{:S(2)}) async-start(f32[1,1,24,64]{2,1,0,3:T(1,128)} %copy.47), calls=%async_computation.2 | async-start | bytes 65536 | tf_op jit(solution)/shard_map/all_to_all | solution.py:74
  109.9 9.4 %copy-start.3 = (bf16[1,24,4,576]{3,2,1,0:T(4,128)(2,1)S(1)}, bf16[1,24,4,576]{3,2,1,0:T(4,128)(2,1)}, u32[]{:S(2)}) copy-start(bf16[1,24,4,576]{3,2,1,0:T(4,128)(2,1)} %param.9) | copy-start | bytes 331780
  109.9 9.5 %copy-start.5 = (s32[1,24]{1,0:T(1,128)S(1)}, s32[1,24]{1,0:T(1,128)}, u32[]{:S(2)}) copy-start(s32[1,24]{1,0:T(1,128)} %param.13) | copy-start | bytes 292
  110.0 15.5 %copy-start.4 = (bf16[1,24,576]{2,1,0:T(8,128)(2,1)S(1)}, bf16[1,24,576]{2,1,0:T(8,128)(2,1)}, u32[]{:S(2)}) copy-start(bf16[1,24,576]{2,1,0:T(8,128)(2,1)} %param.11) | copy-start | bytes 82948
  114.8 63.7 %all-to-all-start = ((f32[16,1,1,24,4,512]{5,4,3,2,1,0:T(4,128)}), f32[16,1,1,24,4,512]{5,4,3,2,1,0:T(4,128)}, u32[]{:S(2)}, u32[]{:S(2)}) async-start(f32[16,1,1,24,4,512]{5,4,3,2,1,0:T(4,128)} %fusion.18), calls=%async_computation | async-start | bytes 6291456 | tf_op jit(solution)/shard_map/all_to_all | solution.py:70
  119.3 149.3 %reduce-scatter.4.cloned.1.call-start = ((), (), s32[]{:S(2)}) async-start(), calls=%async_computation.5 | async-start | bytes 3899392
  119.5 61.7 %copy-start.2 = (bf16[4,512,128]{2,1,0:T(8,128)(2,1)S(1)}, bf16[4,512,128]{2,1,0:T(8,128)(2,1)}, u32[]{:S(2)}) copy-start(bf16[4,512,128]{2,1,0:T(8,128)(2,1)} %param.14) | copy-start | bytes 1572868
Sparse Core Ops, SparseCore 0:
  9.6 43.7 all-gather.1
  189.3 79.2 reduce-scatter.3
